TPU v7x, 256 devices: a whole 4x4x8 slice. The times are simulated.
256 devices in a mesh: dp: 32 (over z, y), row: 2 (over core), col: 4 (over x).
Axes of the slice: x: 4, y: 4, z: 8, core: 2. Of those that a mesh axis runs over, the one named last changes fastest.
Arguments:
- x_input: bfloat16 [32, 32, 64, 640], P('dp', 'row', 'col'), may hold values from -6 to 6
- pre_act: bfloat16 [32, 32, 64, 640], P('dp', 'row', 'col'), may hold values from -6 to 6
- out_grad: bfloat16 [32, 32, 64, 640], P('dp', 'row', 'col'), may hold values from -0.15625 to 0.15625
- conv_weight: bfloat16 [3, 3, 640, 640], replicated, may hold values from -0.078125 to 0.078125
- q_prev: float32 [5760, 2, 64], replicated, may hold values from -6 to 6
Outputs:
- p_basis: float32 [640, 2, 64], P('dp')
- q_next: float32 [5760, 2, 64], P('dp')
All inputs are finite; a program needn't handle non-finite values.
Results may differ from a plain program's by a relative error of at most 0.0036.
Values may be sent and summed in bfloat16 or wider, within the bound.
A program may use at most 128 MiB of HBM per device.

v0:
```python
import jax
import jax.numpy as jnp
from jax import lax
from jax.sharding import PartitionSpec as P


def padded_2(value, sides, width):
    for axis, dim in sides:
        size, length = (lax.axis_size(axis), value.shape[dim])
        up = [(i, (i + 1) % size) for i in range(size - 1)]
        down = [(j, i) for i, j in up]
        last = lax.slice_in_dim(value, length - width, length, axis=dim)
        leading = lax.slice_in_dim(value, 0, width, axis=dim)
        before = lax.ppermute(last, axis, up)
        after = lax.ppermute(leading, axis, down)
        value = jnp.concatenate([before, value, after], axis=dim)
    return value


def silu_slope(pre_float):
    sigma = jax.nn.sigmoid(pre_float)
    return sigma * (1.0 + pre_float * (1.0 - sigma))


def contract_first(left, right, exact):
    if exact:
        return lax.dot_general(
            left,
            right,
            (((0,), (0,)), ((), ())),
            precision=lax.Precision.HIGHEST,
            preferred_element_type=jnp.float32,
        )
    return lax.dot_general(
        left, right, (((0,), (0,)), ((), ())), preferred_element_type=jnp.float32
    )


def tap_window(padded, shift_row, shift_col, height, breadth):
    return padded[
        1 + shift_row : 1 + shift_row + height, 1 + shift_col : 1 + shift_col + breadth, :
    ].reshape(height * breadth, padded.shape[2])


def column_terms(moments, q_prev):
    return jnp.stack(
        [contract_first(moments[layer], q_prev[:, layer, :], True) for layer in range(2)], axis=1
    )


def row_terms(moments, ortho_basis):
    return jnp.stack(
        [
            jnp.dot(
                moments[layer],
                ortho_basis[:, layer, :],
                precision=lax.Precision.HIGHEST,
                preferred_element_type=jnp.float32,
            )
            for layer in range(2)
        ],
        axis=1,
    )


def gram_of(power_raw):
    return jnp.einsum(
        "mqn,mqg->qng",
        power_raw,
        power_raw,
        precision=lax.Precision.HIGHEST,
        preferred_element_type=jnp.float32,
    )


def orthonormal(power_raw, gram_matrix):
    bases = []
    for layer in range(2):
        lower = jnp.linalg.cholesky(gram_matrix[layer])
        bases.append(
            lax.linalg.triangular_solve(
                lower, power_raw[:, layer, :], left_side=False, lower=True, transpose_a=True
            )
        )
    return jnp.stack(bases, axis=1)


def on_device(x_input, pre_act, out_grad, conv_weight, q_prev):
    height, breadth, channels = (x_input.shape[1], x_input.shape[2], x_input.shape[3])
    pixels = height * breadth
    input_tile = x_input.reshape(height, breadth, channels)
    grad_tile = out_grad.reshape(height, breadth, channels)
    pre_float = pre_act.reshape(pixels, channels).astype(jnp.float32)
    hidden_flat = jax.nn.silu(pre_float).astype(jnp.bfloat16)
    grad_pad = padded_2(grad_tile, (("row", 0), ("col", 1)), 1)
    back_grad = jnp.zeros((pixels, channels), jnp.float32)
    second_taps = []
    for shift_row in (-1, 0, 1):
        for shift_col in (-1, 0, 1):
            window = tap_window(grad_pad, -shift_row, -shift_col, height, breadth)
            back_grad = back_grad + lax.dot_general(
                window,
                conv_weight[shift_row + 1, shift_col + 1],
                (((1,), (1,)), ((), ())),
                preferred_element_type=jnp.float32,
            )
            second_taps.append(contract_first(hidden_flat, window, False))
    pre_grad = (back_grad * silu_slope(pre_float)).astype(jnp.bfloat16)
    first_taps = []
    deriv_pad = padded_2(pre_grad.reshape(height, breadth, channels), (("row", 0), ("col", 1)), 1)
    input_flat = input_tile.reshape(pixels, channels)
    for shift_row in (-1, 0, 1):
        for shift_col in (-1, 0, 1):
            first_taps.append(
                contract_first(
                    input_flat,
                    tap_window(deriv_pad, -shift_row, -shift_col, height, breadth),
                    False,
                )
            )
    moments = jnp.stack(
        [
            jnp.stack(first_taps).reshape(9 * channels, channels),
            jnp.stack(second_taps).reshape(9 * channels, channels),
        ]
    )
    kernel_rows = moments.shape[1]
    owner = lax.axis_index("dp")
    basis_count = channels // lax.axis_size("dp")
    factor_count = kernel_rows // lax.axis_size("dp")
    power_raw = lax.psum(column_terms(moments, q_prev), ("dp", "row", "col"))
    ortho_basis = orthonormal(power_raw, gram_of(power_raw))
    factor_full = lax.psum(row_terms(moments, ortho_basis), ("dp", "row", "col"))
    basis_out = lax.dynamic_slice_in_dim(ortho_basis, owner * basis_count, basis_count, 0)
    factor_out = lax.dynamic_slice_in_dim(factor_full, owner * factor_count, factor_count, 0)
    return (basis_out, factor_out)


def solution(mesh):
    placed = (
        P("dp", "row", "col", None),
        P("dp", "row", "col", None),
        P("dp", "row", "col", None),
        P(),
        P(),
    )
    return jax.shard_map(
        on_device,
        mesh=mesh,
        in_specs=placed,
        out_specs=(P("dp", None, None), P("dp", None, None)),
        check_vma=False,
    )
```

profile of v0, /device:TPU:6, one launch (start us, length us, event | category | flops | bytes accessed | tf_op | source)
XLA Modules:
  0.0 655.5 jit_solution(3594010810887087729)
XLA Ops:
  7.2 0.8 slice_bitcast_fusion.9
  8.0 1.3 collective-permute-start.1
  9.3 3.0 collective-permute-start
  12.3 1.2 fusion.43
  13.5 1.2 fusion.38
  14.7 1.1 pad_maximum_fusion.11
  15.8 1.3 collective-permute-start.3
  17.1 4.5 collective-permute-start.2
  21.7 1.1 pad_maximum_fusion.5
  22.8 1.6 fusion.23
  24.5 1.4 maximum_maximum_fusion
  28.5 1.1 slice-done.4
  29.6 1.1 slice-done.5
  36.4 1.4 collective-permute-start.5
  37.8 3.2 collective-permute-start.4
  41.1 8.8 %fusion.12 = f32[640,1,64]{0,2,1:T(8,128)S(1)} fusion(f32[5760,640]{1,0:T(8,128)S(1)} %bitcast.253, f32[5760,2,64]{0,2,1:T(8,128)S(1)} %copy-done.5), kind=kOutput, calls=%fused_computation.38 | convolution fusion | flops 2831155200 | bytes 16384000 | tf_op jit(solution)/shard_map/dot_general | solution.py:27
  50.0 1.3 collective-permute-start.7
  51.3 4.8 collective-permute-start.6
  56.1 1.4 collective-permute-done.6
  62.3 9.2 %fusion.9 = f32[640,1,64]{0,2,1:T(8,128)S(1)} fusion(f32[5760,640]{1,0:T(8,128)S(1)} %bitcast.249, f32[5760,2,64]{0,2,1:T(8,128)S(1)} %copy-done.5), kind=kOutput, calls=%fused_computation.37 | convolution fusion | flops 2831155200 | bytes 16384000 | tf_op jit(solution)/shard_map/dot_general | solution.py:27
  72.3 249.7 %all-reduce.3.cloned.1.call-done = f32[640,2,64]{0,2,1:T(8,128)} async-done(((f32[640,2,64]{0,2,1:T(8,128)}), f32[640,2,64]{0,2,1:T(8,128)}) %all-reduce.3.cloned.1.call-update) | async-done | bytes 327696 | tf_op jit(solution)/shard_map/psum | solution.py:131
  322.0 1.5 fusion.62
  323.8 5.8 cholesky.44
  331.0 4.9 custom-call.6
  335.9 5.9 cholesky.55
  343.1 4.9 custom-call.7
  348.0 1.4 fusion.45
  349.4 17.3 %convolution_bitcast_fusion = f32[5760,1,64]{0,2,1:T(8,128)S(1)} fusion(f32[5760,640]{1,0:T(8,128)} %bitcast.254, f32[64,640]{1,0:T(8,128)S(1)} %fusion.45), kind=kOutput, calls=%fused_computation | convolution fusion | flops 2831155200 | bytes 16384000 | tf_op jit(solution)/shard_map/dot_general | solution.py:54
  367.1 14.2 %convolution_bitcast_fusion.1 = f32[5760,1,64]{0,2,1:T(8,128)S(1)} fusion(f32[5760,640]{1,0:T(8,128)S(1)} %bitcast.252, f32[64,640]{1,0:T(8,128)S(1)} %fusion.46), kind=kOutput, calls=%fused_computation.1 | convolution fusion | flops 2831155200 | bytes 16384000 | tf_op jit(solution)/shard_map/dot_general | solution.py:54
  381.4 1.8 pad_maximum_fusion
  384.0 262.8 %all-reduce.5.cloned.1.call-done = f32[5760,2,64]{0,2,1:T(8,128)} async-done(((f32[5760,2,64]{0,2,1:T(8,128)}), f32[5760,2,64]{0,2,1:T(8,128)}) %all-reduce.5.cloned.1.call-update) | async-done | bytes 2949136 | tf_op jit(solution)/shard_map/psum | solution.py:133
  646.8 1.7 constant_dynamic-slice_fusion
  (84 shorter events, 17.8 us)
Async XLA Ops:
  7.2 50.9 %copy-start = (bf16[1,16,16,640]{3,2,1,0:T(8,128)(2,1)S(1)}, bf16[1,16,16,640]{3,2,1,0:T(8,128)(2,1)}, u32[]{:S(2)}) copy-start(bf16[1,16,16,640]{3,2,1,0:T(8,128)(2,1)} %param.8) | copy-start | bytes 983044
  7.2 314.9 %all-reduce.3.cloned.1.call-start = ((), (), s32[]{:S(2)}) async-start(), calls=%async_computation | async-start | bytes 655360 | tf_op jit(solution)/shard_map/psum | solution.py:131
  8.0 6.7 %collective-permute-start.1 = (bf16[1,16,640]{2,1,0:T(8,128)(2,1)S(1)}, bf16[1,16,640]{2,1,0:T(8,128)(2,1)S(1)}, u32[]{:S(2)}, u32[]{:S(2)}) collective-permute-start(bf16[1,16,640]{2,1,0:T(8,128)(2,1)S(1)} %get-tuple-element.33), channel_id=1, source_target_pairs={{4,0},{5,1},{6,2},{7,3},{12,8},{13,9},{14,10},{15,11},{20,16},{21,... | collective-permute-start | bytes 61448 | tf_op jit(solution)/shard_map/ppermute | solution.py:15
  9.3 5.4 collective-permute-start
  15.8 8.6 %collective-permute-start.3 = (bf16[18,1,640]{2,1,0:T(2,128)(2,1)S(1)}, bf16[18,1,640]{2,1,0:T(2,128)(2,1)S(1)}, u32[]{:S(2)}, u32[]{:S(2)}) collective-permute-start(bf16[18,1,640]{2,1,0:T(2,128)(2,1)S(1)} %get-tuple-element.24), channel_id=1, source_target_pairs={{0,1},{1,2},{2,3},{4,5},{5,6},{6,7},{8,9},{9,10},{10,11},{12,13},{... | collective-permute-start | bytes 69128 | tf_op jit(solution)/shard_map/ppermute | solution.py:14
  17.1 7.3 %collective-permute-start.2 = (bf16[18,1,640]{2,1,0:T(2,128)(2,1)S(1)}, bf16[18,1,640]{2,1,0:T(2,128)(2,1)S(1)}, u32[]{:S(2)}, u32[]{:S(2)}) collective-permute-start(bf16[18,1,640]{2,1,0:T(2,128)(2,1)S(1)} %get-tuple-element.25), channel_id=1, source_target_pairs={{1,0},{2,1},{3,2},{5,4},{6,5},{7,6},{9,8},{10,9},{11,10},{13,12},{... | collective-permute-start | bytes 69128 | tf_op jit(solution)/shard_map/ppermute | solution.py:15
  24.4 3.5 copy-start.3
  24.4 3.5 copy-start.6
  27.4 2.2 slice-start.4
  27.9 2.8 slice-start.5
  33.1 8.0 %copy-start.2 = (f32[9,640,640]{2,1,0:T(8,128)}, f32[9,640,640]{2,1,0:T(8,128)S(1)}, u32[]{:S(2)}) copy-start(f32[9,640,640]{2,1,0:T(8,128)S(1)} %bitcast_dynamic-update-slice_fusion.9) | copy-start | bytes 44236804
  33.5 7.5 %copy-start.5 = (f32[5760,2,64]{0,2,1:T(8,128)S(1)}, f32[5760,2,64]{0,2,1:T(8,128)}, u32[]{:S(2)}) copy-start(f32[5760,2,64]{0,2,1:T(8,128)} %param.12) | copy-start | bytes 8847364
  36.4 13.5 %collective-permute-start.5 = (bf16[1,16,640]{2,1,0:T(8,128)(2,1)S(1)}, bf16[1,16,640]{2,1,0:T(8,128)(2,1)S(1)}, u32[]{:S(2)}, u32[]{:S(2)}) collective-permute-start(bf16[1,16,640]{2,1,0:T(8,128)(2,1)S(1)} %get-tuple-element.29), channel_id=1, source_target_pairs={{4,0},{5,1},{6,2},{7,3},{12,8},{13,9},{14,10},{15,11},{20,16},{21,... | collective-permute-start | bytes 61448 | tf_op jit(solution)/shard_map/ppermute | solution.py:15
  37.8 12.1 %collective-permute-start.4 = (bf16[1,16,640]{2,1,0:T(8,128)(2,1)S(1)}, bf16[1,16,640]{2,1,0:T(8,128)(2,1)S(1)}, u32[]{:S(2)}, u32[]{:S(2)}) collective-permute-start(bf16[1,16,640]{2,1,0:T(8,128)(2,1)S(1)} %get-tuple-element.28), channel_id=1, source_target_pairs={{0,4},{1,5},{2,6},{3,7},{8,12},{9,13},{10,14},{11,15},{16,20},{17,... | collective-permute-start | bytes 61448 | tf_op jit(solution)/shard_map/ppermute | solution.py:14
  50.0 6.1 collective-permute-start.7
  51.3 6.3 collective-permute-start.6
  62.3 9.3 %copy-start.1 = (f32[9,640,640]{2,1,0:T(8,128)}, f32[9,640,640]{2,1,0:T(8,128)S(1)}, u32[]{:S(2)}) copy-start(f32[9,640,640]{2,1,0:T(8,128)S(1)} %bitcast_dynamic-update-slice_fusion) | copy-start | bytes 44236804
  72.3 574.5 %all-reduce.5.cloned.1.call-start = ((), (), s32[]{:S(2)}) async-start(), calls=%async_computation.1 | async-start | bytes 5898240 | tf_op jit(solution)/shard_map/psum | solution.py:133
  348.0 19.1 %slice-start = ((s8[14745600]{0:T(1024)(128)(4,1)}), s8[4194304]{0:T(1024)(128)(4,1)S(1)}, s32[]{:S(2)}) async-start(s8[14745600]{0:T(1024)(128)(4,1)} %bitcast.250), calls=%async_computation.2 | async-start | bytes 8388608
  349.4 17.3 %copy-start.4 = (f32[640,2,64]{0,2,1:T(8,128)S(1)}, f32[640,2,64]{0,2,1:T(8,128)}, u32[]{:S(2)}) copy-start(f32[640,2,64]{0,2,1:T(8,128)} %all-reduce.3.cloned.1.call-done) | copy-start | bytes 983044
  349.4 17.7 %slice-start.1 = ((s8[14745600]{0:T(1024)(128)(4,1)}), s8[4194304]{0:T(1024)(128)(4,1)S(1)}, s32[]{:S(2)}) async-start(s8[14745600]{0:T(1024)(128)(4,1)} %bitcast.250), calls=%async_computation.3 | async-start | bytes 8388608
  349.4 17.7 %slice-start.2 = ((s8[14745600]{0:T(1024)(128)(4,1)}), s8[4194304]{0:T(1024)(128)(4,1)S(1)}, s32[]{:S(2)}) async-start(s8[14745600]{0:T(1024)(128)(4,1)} %bitcast.250), calls=%async_computation.4 | async-start | bytes 8388608
  349.4 17.7 %slice-start.3 = ((s8[14745600]{0:T(1024)(128)(4,1)}), s8[2162688]{0:T(1024)(128)(4,1)S(1)}, s32[]{:S(2)}) async-start(s8[14745600]{0:T(1024)(128)(4,1)} %bitcast.250), calls=%async_computation.5 | async-start | bytes 4325376
Sparse Core Ops, SparseCore 0:
  72.4 249.5 all-reduce.2
  383.3 263.3 all-reduce.4
where the time goes:
time: 662 us; the launch traced here: 655 us
  waiting for transfers between devices  514 us (78%)
  matrix products  66.6 us (10%)
  other arithmetic  33.2 us (5%)
  starting transfers between devices  20.9 us (3%)
  between operations  14.8 us (2%)
    psum x1, waiting for transfers between devices, on_device(): lax.psum(row_terms(moments, ortho_basis), ('dp', 'row', 'col'))  263 us
    psum x1, waiting for transfers between devices, on_device(): power_raw = lax.psum(column_terms(moments, q_prev), ('dp', 'row', 'col'))  250 us
    dot_general x2, matrix products, row_terms(): jnp.dot(moments[layer], ortho_basis[:, layer, :], precision=lax.Precision...  31.5 us
    dot_general x2, matrix products, contract_first(): lax.dot_general(left, right, (((0,), (0,)), ((), ())), precision=lax.Prec...  18.1 us
  transfers between devices with their start and end apart: 10, of which 3 were waited for; matrix products, arithmetic and copies ran while one was open for 2% of the time, Pallas kernels for 0%

commit v1 on v0

--- a/solution.py
+++ b/solution.py
@@ -128,7 +128,7 @@
     owner = lax.axis_index("dp")
     basis_count = channels // lax.axis_size("dp")
     factor_count = kernel_rows // lax.axis_size("dp")
-    power_raw = lax.psum(column_terms(moments, q_prev), ("dp", "row", "col"))
+    power_raw = lax.psum(lax.psum(column_terms(moments, q_prev), ("row", "col")), "dp")
     ortho_basis = orthonormal(power_raw, gram_of(power_raw))
     factor_full = lax.psum(row_terms(moments, ortho_basis), ("dp", "row", "col"))
     basis_out = lax.dynamic_slice_in_dim(ortho_basis, owner * basis_count, basis_count, 0)

time: 662 us -> 629 us (0.950)
  waiting for transfers between devices: 514 us -> 481 us
    psum x1 -> x2, waiting for transfers between devices: 250 us -> 218 us  [the longest x1 150 us: on_device(): lax.psum(lax.psum(column_terms(moments, q_prev), ('row', 'col')), 'dp')]
  transfers between devices with their start and end apart: 10 -> 11, of which waited for: 3 -> 4; matrix products, arithmetic and copies ran while one was open for 2% -> 2% of each run, Pallas kernels for 0% -> 0%
where the time goes in v1:
time: 629 us; the launch traced here: 622 us
  waiting for transfers between devices  481 us (76%)
  matrix products  66.6 us (11%)
  other arithmetic  33.2 us (5%)
  starting transfers between devices  20.9 us (3%)
  between operations  14.6 us (2%)
    psum x1, waiting for transfers between devices, on_device(): lax.psum(row_terms(moments, ortho_basis), ('dp', 'row', 'col'))  261 us
    psum x1, waiting for transfers between devices, on_device(): lax.psum(lax.psum(column_terms(moments, q_prev), ('row', 'col')), 'dp')  150 us
    psum x1, waiting for transfers between devices, on_device(): lax.psum(column_terms(moments, q_prev), ('row', 'col'))  67.5 us
    dot_general x2, matrix products, row_terms(): jnp.dot(moments[layer], ortho_basis[:, layer, :], precision=lax.Precision...  31.5 us
    dot_general x2, matrix products, contract_first(): lax.dot_general(left, right, (((0,), (0,)), ((), ())), precision=lax.Prec...  18.1 us
    another operation x6, other arithmetic, orthonormal(): lower = jnp.linalg.cholesky(gram_matrix[layer])  13.1 us
  transfers between devices with their start and end apart: 11, of which 4 were waited for; matrix products, arithmetic and copies ran while one was open for 2% of the time, Pallas kernels for 0%

profile of v1, /device:TPU:6, one launch (start us, length us, event | category | flops | bytes accessed | tf_op | source)
XLA Modules:
  0.0 622.1 jit_solution(15925280872473161942)
XLA Ops:
  8.0 1.3 collective-permute-start.1
  9.3 3.0 collective-permute-start
  12.3 1.2 fusion.43
  13.5 1.2 fusion.38
  14.7 1.1 pad_maximum_fusion.11
  15.8 1.3 collective-permute-start.3
  17.1 4.5 collective-permute-start.2
  21.7 1.1 pad_maximum_fusion.5
  22.8 1.6 fusion.23
  24.5 1.4 maximum_maximum_fusion
  28.5 1.1 slice-done.4
  29.6 1.1 slice-done.5
  36.4 1.4 collective-permute-start.5
  37.8 3.2 collective-permute-start.4
  41.1 8.8 %fusion.12 = f32[640,1,64]{0,2,1:T(8,128)S(1)} fusion(f32[5760,640]{1,0:T(8,128)S(1)} %bitcast.253, f32[5760,2,64]{0,2,1:T(8,128)S(1)} %copy-done.5), kind=kOutput, calls=%fused_computation.38 | convolution fusion | flops 2831155200 | bytes 16384000 | tf_op jit(solution)/shard_map/dot_general | solution.py:27
  50.0 1.3 collective-permute-start.7
  51.3 4.8 collective-permute-start.6
  56.1 1.4 collective-permute-done.6
  62.3 9.2 %fusion.9 = f32[640,1,64]{0,2,1:T(8,128)S(1)} fusion(f32[5760,640]{1,0:T(8,128)S(1)} %bitcast.249, f32[5760,2,64]{0,2,1:T(8,128)S(1)} %copy-done.5), kind=kOutput, calls=%fused_computation.37 | convolution fusion | flops 2831155200 | bytes 16384000 | tf_op jit(solution)/shard_map/dot_general | solution.py:27
  72.3 67.5 %all-reduce.4.cloned.1.call-done = f32[640,2,64]{0,2,1:T(8,128)} async-done(((f32[640,2,64]{0,2,1:T(8,128)}), f32[640,2,64]{0,2,1:T(8,128)}) %all-reduce.4.cloned.1.call-update) | async-done | bytes 327696 | tf_op jit(solution)/shard_map/psum | solution.py:131
  139.9 150.4 %all-reduce.6.cloned.1.call-done = f32[640,2,64]{0,2,1:T(8,128)} async-done(((f32[640,2,64]{0,2,1:T(8,128)}), f32[640,2,64]{0,2,1:T(8,128)}) %all-reduce.6.cloned.1.call-update) | async-done | bytes 327696 | tf_op jit(solution)/shard_map/psum | solution.py:131
  290.4 1.5 fusion.62
  292.1 5.8 cholesky.44
  299.3 4.9 custom-call.6
  304.2 5.9 cholesky.55
  311.4 4.9 custom-call.7
  316.3 1.4 fusion.45
  317.7 17.3 %convolution_bitcast_fusion = f32[5760,1,64]{0,2,1:T(8,128)S(1)} fusion(f32[5760,640]{1,0:T(8,128)} %bitcast.254, f32[64,640]{1,0:T(8,128)S(1)} %fusion.45), kind=kOutput, calls=%fused_computation | convolution fusion | flops 2831155200 | bytes 16384000 | tf_op jit(solution)/shard_map/dot_general | solution.py:54
  335.5 14.2 %convolution_bitcast_fusion.1 = f32[5760,1,64]{0,2,1:T(8,128)S(1)} fusion(f32[5760,640]{1,0:T(8,128)S(1)} %bitcast.252, f32[64,640]{1,0:T(8,128)S(1)} %fusion.46), kind=kOutput, calls=%fused_computation.1 | convolution fusion | flops 2831155200 | bytes 16384000 | tf_op jit(solution)/shard_map/dot_general | solution.py:54
  349.7 1.8 pad_maximum_fusion
  352.3 261.4 %all-reduce.8.cloned.1.call-done = f32[5760,2,64]{0,2,1:T(8,128)} async-done(((f32[5760,2,64]{0,2,1:T(8,128)}), f32[5760,2,64]{0,2,1:T(8,128)}) %all-reduce.8.cloned.1.call-update) | async-done | bytes 2949136 | tf_op jit(solution)/shard_map/psum | solution.py:133
  613.7 1.7 constant_dynamic-slice_fusion
  (87 shorter events, 18.7 us)
Async XLA Ops:
  7.2 50.9 %copy-start = (bf16[1,16,16,640]{3,2,1,0:T(8,128)(2,1)S(1)}, bf16[1,16,16,640]{3,2,1,0:T(8,128)(2,1)}, u32[]{:S(2)}) copy-start(bf16[1,16,16,640]{3,2,1,0:T(8,128)(2,1)} %param.8) | copy-start | bytes 983044
  7.2 132.7 %all-reduce.4.cloned.1.call-start = ((), (), s32[]{:S(2)}) async-start(), calls=%async_computation | async-start | bytes 655360 | tf_op jit(solution)/shard_map/psum | solution.py:131
  8.0 6.7 %collective-permute-start.1 = (bf16[1,16,640]{2,1,0:T(8,128)(2,1)S(1)}, bf16[1,16,640]{2,1,0:T(8,128)(2,1)S(1)}, u32[]{:S(2)}, u32[]{:S(2)}) collective-permute-start(bf16[1,16,640]{2,1,0:T(8,128)(2,1)S(1)} %get-tuple-element.33), channel_id=1, source_target_pairs={{4,0},{5,1},{6,2},{7,3},{12,8},{13,9},{14,10},{15,11},{20,16},{21,... | collective-permute-start | bytes 61448 | tf_op jit(solution)/shard_map/ppermute | solution.py:15
  9.3 5.4 collective-permute-start
  15.8 8.6 %collective-permute-start.3 = (bf16[18,1,640]{2,1,0:T(2,128)(2,1)S(1)}, bf16[18,1,640]{2,1,0:T(2,128)(2,1)S(1)}, u32[]{:S(2)}, u32[]{:S(2)}) collective-permute-start(bf16[18,1,640]{2,1,0:T(2,128)(2,1)S(1)} %get-tuple-element.24), channel_id=1, source_target_pairs={{0,1},{1,2},{2,3},{4,5},{5,6},{6,7},{8,9},{9,10},{10,11},{12,13},{... | collective-permute-start | bytes 69128 | tf_op jit(solution)/shard_map/ppermute | solution.py:14
  17.1 7.3 %collective-permute-start.2 = (bf16[18,1,640]{2,1,0:T(2,128)(2,1)S(1)}, bf16[18,1,640]{2,1,0:T(2,128)(2,1)S(1)}, u32[]{:S(2)}, u32[]{:S(2)}) collective-permute-start(bf16[18,1,640]{2,1,0:T(2,128)(2,1)S(1)} %get-tuple-element.25), channel_id=1, source_target_pairs={{1,0},{2,1},{3,2},{5,4},{6,5},{7,6},{9,8},{10,9},{11,10},{13,12},{... | collective-permute-start | bytes 69128 | tf_op jit(solution)/shard_map/ppermute | solution.py:15
  24.4 3.5 copy-start.3
  24.4 3.5 copy-start.6
  27.4 2.2 slice-start.4
  27.9 2.8 slice-start.5
  33.1 8.0 %copy-start.2 = (f32[9,640,640]{2,1,0:T(8,128)}, f32[9,640,640]{2,1,0:T(8,128)S(1)}, u32[]{:S(2)}) copy-start(f32[9,640,640]{2,1,0:T(8,128)S(1)} %bitcast_dynamic-update-slice_fusion.9) | copy-start | bytes 44236804
  33.5 7.5 %copy-start.5 = (f32[5760,2,64]{0,2,1:T(8,128)S(1)}, f32[5760,2,64]{0,2,1:T(8,128)}, u32[]{:S(2)}) copy-start(f32[5760,2,64]{0,2,1:T(8,128)} %param.12) | copy-start | bytes 8847364
  36.4 13.5 %collective-permute-start.5 = (bf16[1,16,640]{2,1,0:T(8,128)(2,1)S(1)}, bf16[1,16,640]{2,1,0:T(8,128)(2,1)S(1)}, u32[]{:S(2)}, u32[]{:S(2)}) collective-permute-start(bf16[1,16,640]{2,1,0:T(8,128)(2,1)S(1)} %get-tuple-element.29), channel_id=1, source_target_pairs={{4,0},{5,1},{6,2},{7,3},{12,8},{13,9},{14,10},{15,11},{20,16},{21,... | collective-permute-start | bytes 61448 | tf_op jit(solution)/shard_map/ppermute | solution.py:15
  37.8 12.1 %collective-permute-start.4 = (bf16[1,16,640]{2,1,0:T(8,128)(2,1)S(1)}, bf16[1,16,640]{2,1,0:T(8,128)(2,1)S(1)}, u32[]{:S(2)}, u32[]{:S(2)}) collective-permute-start(bf16[1,16,640]{2,1,0:T(8,128)(2,1)S(1)} %get-tuple-element.28), channel_id=1, source_target_pairs={{0,4},{1,5},{2,6},{3,7},{8,12},{9,13},{10,14},{11,15},{16,20},{17,... | collective-permute-start | bytes 61448 | tf_op jit(solution)/shard_map/ppermute | solution.py:14
  50.0 6.1 collective-permute-start.7
  51.3 6.3 %collective-permute-start.6 = (bf16[18,1,640]{2,1,0:T(2,128)(2,1)S(1)}, bf16[18,1,640]{2,1,0:T(2,128)(2,1)S(1)}, u32[]{:S(2)}, u32[]{:S(2)}) collective-permute-start(bf16[18,1,640]{2,1,0:T(2,128)(2,1)S(1)} %get-tuple-element.21), channel_id=1, source_target_pairs={{1,0},{2,1},{3,2},{5,4},{6,5},{7,6},{9,8},{10,9},{11,10},{13,12},{... | collective-permute-start | bytes 69128 | tf_op jit(solution)/shard_map/ppermute | solution.py:15
  62.3 9.3 %copy-start.1 = (f32[9,640,640]{2,1,0:T(8,128)}, f32[9,640,640]{2,1,0:T(8,128)S(1)}, u32[]{:S(2)}) copy-start(f32[9,640,640]{2,1,0:T(8,128)S(1)} %bitcast_dynamic-update-slice_fusion) | copy-start | bytes 44236804
  72.3 218.1 %all-reduce.6.cloned.1.call-start = ((), (), s32[]{:S(2)}) async-start(), calls=%async_computation.1 | async-start | bytes 655360 | tf_op jit(solution)/shard_map/psum | solution.py:131
  139.9 473.8 %all-reduce.8.cloned.1.call-start = ((), (), s32[]{:S(2)}) async-start(), calls=%async_computation.2 | async-start | bytes 5898240 | tf_op jit(solution)/shard_map/psum | solution.py:133
  316.3 19.1 %slice-start = ((s8[14745600]{0:T(1024)(128)(4,1)}), s8[4194304]{0:T(1024)(128)(4,1)S(1)}, s32[]{:S(2)}) async-start(s8[14745600]{0:T(1024)(128)(4,1)} %bitcast.250), calls=%async_computation.3 | async-start | bytes 8388608
  317.7 17.3 %copy-start.4 = (f32[640,2,64]{0,2,1:T(8,128)S(1)}, f32[640,2,64]{0,2,1:T(8,128)}, u32[]{:S(2)}) copy-start(f32[640,2,64]{0,2,1:T(8,128)} %all-reduce.6.cloned.1.call-done) | copy-start | bytes 983044
  317.7 17.7 %slice-start.1 = ((s8[14745600]{0:T(1024)(128)(4,1)}), s8[4194304]{0:T(1024)(128)(4,1)S(1)}, s32[]{:S(2)}) async-start(s8[14745600]{0:T(1024)(128)(4,1)} %bitcast.250), calls=%async_computation.4 | async-start | bytes 8388608
  317.7 17.7 %slice-start.2 = ((s8[14745600]{0:T(1024)(128)(4,1)}), s8[4194304]{0:T(1024)(128)(4,1)S(1)}, s32[]{:S(2)}) async-start(s8[14745600]{0:T(1024)(128)(4,1)} %bitcast.250), calls=%async_computation.5 | async-start | bytes 8388608
  317.7 17.7 %slice-start.3 = ((s8[14745600]{0:T(1024)(128)(4,1)}), s8[2162688]{0:T(1024)(128)(4,1)S(1)}, s32[]{:S(2)}) async-start(s8[14745600]{0:T(1024)(128)(4,1)} %bitcast.250), calls=%async_computation.6 | async-start | bytes 4325376
Sparse Core Ops, SparseCore 0:
  72.4 67.3 all-reduce.3
  143.7 146.6 all-reduce.5
  351.6 261.9 all-reduce.7
